TPU v7x, 32 devices: a whole 2x2x4 slice. The times are simulated.
32 devices in a mesh: row: 4 (over x, core), col: 8 (over z, y).
Axes of the slice: x: 2, y: 2, z: 4, core: 2. Of those that a mesh axis runs over, the one named last changes fastest.
Arguments:
- inputs: bfloat16 [4096, 2048], P(('row', 'col')), may hold values from -6 to 6
- cotangent: bfloat16 [4096, 2048], P(('row', 'col')), may hold values from -12 to 12
- attn_gain: bfloat16 [2048], replicated, may hold values from 0.5 to 1.5
- mlp_gain: bfloat16 [2048], replicated, may hold values from 0.5 to 1.5
- attn_router: bfloat16 [2048, 4], replicated, may hold values from -0.09375 to 0.09375
- mlp_router: bfloat16 [2048, 4], replicated, may hold values from -0.09375 to 0.09375
- kv_weight: bfloat16 [4096, 2048], P(('row', 'col')), may hold values from -0.125 to 0.125
- query_weight: bfloat16 [4, 2048, 2048], P('row'), may hold values from -0.125 to 0.125
- output_weight: bfloat16 [4, 2048, 2048], P('row'), may hold values from -1 to 1
- expert_weight: bfloat16 [4, 5632, 3, 2048], P('row', 'col'), may hold values from -0.125 to 0.125
- attn_routes: int32 [4, 1024, 2], P(None, 'col'), may hold values from 0 to 3, all different within a row
- mlp_routes: int32 [4, 1024, 2], P(None, 'col'), may hold values from 0 to 3, all different within a row
- prefix_len: int32 [4, 8], P(None, 'col'), may hold values from 0 to 128
Outputs:
- output: bfloat16 [4096, 2048], P(('row', 'col'))
- input_grad: float32 [4096, 2048], P(('row', 'col'))
- attn_gain_grad: float32 [2048], replicated
- mlp_gain_grad: float32 [2048], replicated
- attn_router_grad: float32 [2048, 4], replicated
- mlp_router_grad: float32 [2048, 4], replicated
- kv_weight_grad: float32 [4096, 2048], P(('row', 'col'))
- query_weight_grad: float32 [4, 2048, 2048], P('row', 'col')
- out_weight_grad: float32 [4, 2048, 2048], P('row', 'col')
- expert_weight_grad: float32 [4, 5632, 3, 2048], P('row', 'col')
All inputs are finite; a program needn't handle non-finite values.
Results may differ from a plain program's by a relative error of at most 0.02.
Values may be sent and summed in bfloat16 or wider, within the bound.
No kernel may reach another device: no remote copies, remote signals or barrier semaphores. Data moves between devices by JAX's collectives and lax.ppermute only.
A program may use at most 576 MiB of HBM per device.

v0:
```python
import jax
import jax.numpy as jnp
from jax import lax
from jax.sharding import PartitionSpec as P

HEAD_DIM = 128
TOP = 2


eps = 1e-06
theta = 10000.0
far_below = -1e30
precise = lax.Precision.HIGHEST


def normalize(values, gain_vector):
    inverse = lax.rsqrt(jnp.mean(values * values, axis=-1, keepdims=True) + eps)
    return (values * inverse * gain_vector, inverse)


def normalize_back(values, inverse, gain_vector, upstream):
    scaled = upstream * gain_vector
    gain_term = jnp.sum(upstream * values * inverse, axis=0)
    inner_mean = jnp.mean(scaled * values, axis=-1, keepdims=True)
    return (inverse * scaled - values * inverse * inverse * inverse * inner_mean, gain_term)


def rotary_tables(positions):
    half_dim = HEAD_DIM // 2
    frequency = theta ** (-jnp.arange(half_dim, dtype=jnp.float32) / half_dim)
    angles = positions.astype(jnp.float32)[..., None, None] * frequency
    return (jnp.cos(angles), jnp.sin(angles))


def rotate(values, cosine, sine_table):
    half_dim = HEAD_DIM // 2
    front_half = values[..., :half_dim]
    back_half = values[..., half_dim:]
    return jnp.concatenate(
        [
            front_half * cosine - back_half * sine_table,
            front_half * sine_table + back_half * cosine,
        ],
        axis=-1,
    )


def rotate_back(gradient, cosine, sine_table):
    half_dim = HEAD_DIM // 2
    front_half = gradient[..., :half_dim]
    back_half = gradient[..., half_dim:]
    return jnp.concatenate(
        [
            front_half * cosine + back_half * sine_table,
            back_half * cosine - front_half * sine_table,
        ],
        axis=-1,
    )


def slot_places(routes, capacity, experts):
    flat_routes = routes.reshape(-1)
    onehot = (flat_routes[:, None] == jnp.arange(experts, dtype=jnp.int32)[None, :]).astype(
        jnp.int32
    )
    before = jnp.cumsum(onehot, axis=0) - onehot
    slot_rank = jnp.sum(before * onehot, axis=1)
    return jnp.where(slot_rank < capacity, flat_routes * capacity + slot_rank, experts * capacity)


def slot_positions(places, length, slot_count):
    anchor = jnp.repeat(jnp.arange(length, dtype=jnp.int32), TOP)
    return jnp.zeros((slot_count + 1,), jnp.int32).at[places].set(anchor)[:slot_count]


def pair_gates(logits, routes):
    chosen = jnp.take_along_axis(logits, routes, axis=1)
    highest = jnp.max(chosen, axis=1, keepdims=True)
    weights = jnp.exp(chosen - highest)
    return weights / jnp.sum(weights, axis=1, keepdims=True)


def gates_back(gates, gate_grads, routes, experts):
    chosen_grad = gates * (gate_grads - jnp.sum(gates * gate_grads, axis=1, keepdims=True))
    route_table = (
        routes[:, :, None] == jnp.arange(experts, dtype=jnp.int32)[None, None, :]
    ).astype(jnp.float32)
    return jnp.sum(chosen_grad[:, :, None] * route_table, axis=1)


def dispatch(pair_rows, places, slot_count):
    return (
        jnp.zeros((slot_count + 1, pair_rows.shape[1]), pair_rows.dtype)
        .at[places]
        .set(pair_rows)[:slot_count]
    )


def combine(returned, places):
    padded = jnp.concatenate([returned, jnp.zeros((1, returned.shape[1]), returned.dtype)], axis=0)
    return padded[places].reshape(-1, TOP, returned.shape[1])


def trade(buffer):
    return lax.all_to_all(buffer, "row", split_axis=0, concat_axis=0, tiled=True)


def contract_rows(left, right):
    return lax.dot_general(
        left, right, (((0,), (0,)), ((), ())), preferred_element_type=jnp.float32
    )


def contract_cols(left, right):
    return lax.dot_general(
        left, right, (((1,), (1,)), ((), ())), preferred_element_type=jnp.float32
    )


def local(
    inputs,
    cotangent,
    attn_gain,
    mlp_gain,
    attn_router,
    mlp_router,
    kv_weight,
    query_weight,
    output_weight,
    expert_weight,
    attn_routes,
    mlp_routes,
    prefix_len,
):
    length, model_width = inputs.shape
    experts = lax.axis_size("row")
    own_row = lax.axis_index("row")
    capacity = length * TOP // experts
    slot_count = experts * capacity
    head_width = query_weight.shape[2]
    head_count = head_width // HEAD_DIM
    score_scale = HEAD_DIM ** (-0.5)
    positions = jnp.arange(length, dtype=jnp.int32)
    cos_own, sin_own = rotary_tables(positions)
    own_attn = lax.dynamic_index_in_dim(attn_routes, own_row, 0, keepdims=False)
    own_mlp = lax.dynamic_index_in_dim(mlp_routes, own_row, 0, keepdims=False)
    places_attn = slot_places(own_attn, capacity, experts)
    places_mlp = slot_places(own_mlp, capacity, experts)

    def source_slots(routes):
        return slot_positions(slot_places(routes, capacity, experts), length, slot_count)

    source_pos = jax.vmap(source_slots)(attn_routes)
    arrived_pos = lax.dynamic_slice_in_dim(source_pos, own_row * capacity, capacity, 1)
    prefixes = prefix_len[:, 0]
    allowed = (positions[None, None, :] <= arrived_pos[:, :, None]) | (
        positions[None, None, :] < prefixes[:, None, None]
    )
    allowed = allowed[:, None]
    cos_slot, sin_slot = rotary_tables(arrived_pos)
    tokens = inputs.astype(jnp.float32)
    gain_attn = attn_gain.astype(jnp.float32)
    gain_mlp = mlp_gain.astype(jnp.float32)
    router_attn = attn_router.astype(jnp.float32)
    router_mlp = mlp_router.astype(jnp.float32)
    normed, inverse_attn = normalize(tokens, gain_attn)
    normed_low = normed.astype(jnp.bfloat16)
    gates_attn = pair_gates(
        jnp.dot(normed_low, attn_router, preferred_element_type=jnp.float32), own_attn
    )
    kv_whole = lax.all_gather(kv_weight, ("row", "col"), axis=0, tiled=True)
    projected = contract_cols(normed_low, kv_whole)
    keys_low = rotate(
        projected[:, :head_width].reshape(length, head_count, HEAD_DIM), cos_own, sin_own
    )
    keys_low = keys_low.astype(jnp.bfloat16).reshape(length, head_width)
    values_low = projected[:, head_width:].astype(jnp.bfloat16)
    keys_all, values_all = (
        lax.all_gather(keys_low, "row", axis=0, tiled=True),
        lax.all_gather(values_low, "row", axis=0, tiled=True),
    )
    keys_all = keys_all.reshape(experts, length, head_count, HEAD_DIM)
    values_all = values_all.reshape(experts, length, head_count, HEAD_DIM)
    sent_attn = dispatch(jnp.repeat(normed_low, TOP, axis=0), places_attn, slot_count)
    arrived = trade(sent_attn.reshape(experts, capacity, model_width)).reshape(
        slot_count, model_width
    )
    query_pre = jnp.dot(arrived, query_weight[0], preferred_element_type=jnp.float32)
    queries = rotate(
        query_pre.reshape(experts, capacity, head_count, HEAD_DIM), cos_slot, sin_slot
    ).astype(jnp.bfloat16)

    def masked_scores():
        raw_scores = (
            jnp.einsum("schd,slhd->shcl", queries, keys_all, preferred_element_type=jnp.float32)
            * score_scale
        )
        return jnp.where(allowed, raw_scores, far_below)

    masked = masked_scores()
    row_peak = jnp.max(masked, axis=-1, keepdims=True)
    exponent = jnp.exp(masked - row_peak)
    row_total = jnp.sum(exponent, axis=-1, keepdims=True)
    log_total = row_peak + jnp.log(row_total)
    attention = exponent / row_total
    attended = jnp.einsum(
        "shcl,slhd->schd",
        attention.astype(jnp.bfloat16),
        values_all,
        preferred_element_type=jnp.float32,
    )
    attended = attended.reshape(slot_count, head_width).astype(jnp.bfloat16)
    answers = jnp.dot(attended, output_weight[0], preferred_element_type=jnp.float32).astype(
        jnp.bfloat16
    )
    returned = trade(answers.reshape(experts, capacity, model_width)).reshape(
        slot_count, model_width
    )
    pairs_attn = combine(returned, places_attn).astype(jnp.float32)
    mixed = tokens + jnp.sum(gates_attn[:, :, None] * pairs_attn, axis=1)
    normed_mlp, inverse_mlp = normalize(mixed, gain_mlp)
    normed_mlp_low = normed_mlp.astype(jnp.bfloat16)
    gates_mlp = pair_gates(
        jnp.dot(normed_mlp_low, mlp_router, preferred_element_type=jnp.float32), own_mlp
    )
    sent_mlp = dispatch(jnp.repeat(normed_mlp_low, TOP, axis=0), places_mlp, slot_count)
    arrived_mlp = trade(sent_mlp.reshape(experts, capacity, model_width)).reshape(
        slot_count, model_width
    )
    local_weight = expert_weight[0]
    gathered = lax.all_gather(local_weight, "col", axis=0, tiled=True)
    gate_pre = contract_cols(arrived_mlp, gathered[:, 0])
    up_pre = contract_cols(arrived_mlp, gathered[:, 1])
    sigmoid_gate = jax.nn.sigmoid(gate_pre)
    hidden = (gate_pre * sigmoid_gate * up_pre).astype(jnp.bfloat16)
    down_out = jnp.dot(hidden, gathered[:, 2], preferred_element_type=jnp.float32).astype(
        jnp.bfloat16
    )
    back_down = trade(down_out.reshape(experts, capacity, model_width)).reshape(
        slot_count, model_width
    )
    pairs_mlp = combine(back_down, places_mlp).astype(jnp.float32)
    output = (mixed + jnp.sum(gates_mlp[:, :, None] * pairs_mlp, axis=1)).astype(jnp.bfloat16)
    upstream = cotangent.astype(jnp.float32)
    pair_grad_mlp = (gates_mlp[:, :, None] * upstream[:, None, :]).astype(jnp.bfloat16)
    gate_grad_mlp = jnp.sum(pairs_mlp * upstream[:, None, :], axis=-1)
    sent_grad = dispatch(pair_grad_mlp.reshape(length * TOP, model_width), places_mlp, slot_count)
    down_grad = trade(sent_grad.reshape(experts, capacity, model_width)).reshape(
        slot_count, model_width
    )
    hidden_grad = contract_cols(down_grad, gathered[:, 2])
    gate_grad = (
        hidden_grad * up_pre * sigmoid_gate * (1.0 + gate_pre * (1.0 - sigmoid_gate))
    ).astype(jnp.bfloat16)
    up_grad = (hidden_grad * gate_pre * sigmoid_gate).astype(jnp.bfloat16)
    expert_term = lax.psum_scatter(
        jnp.stack(
            [
                contract_rows(gate_grad, arrived_mlp),
                contract_rows(up_grad, arrived_mlp),
                contract_rows(hidden, down_grad),
            ],
            axis=1,
        ).astype(jnp.bfloat16),
        "col",
        scatter_dimension=0,
        tiled=True,
    ).astype(jnp.float32)
    slot_grad = jnp.dot(gate_grad, gathered[:, 0], preferred_element_type=jnp.float32)
    slot_grad = (
        slot_grad + jnp.dot(up_grad, gathered[:, 1], preferred_element_type=jnp.float32)
    ).astype(jnp.bfloat16)
    back_mlp = trade(slot_grad.reshape(experts, capacity, model_width)).reshape(
        slot_count, model_width
    )
    normed_mlp_grad = jnp.sum(combine(back_mlp, places_mlp).astype(jnp.float32), axis=1)
    logit_grad_mlp = gates_back(gates_mlp, gate_grad_mlp, own_mlp, experts)
    normed_mlp_grad = normed_mlp_grad + jnp.dot(logit_grad_mlp, router_mlp.T, precision=precise)
    router_mlp_term = jnp.dot(
        normed_mlp_low.astype(jnp.float32).T, logit_grad_mlp, precision=precise
    )
    mixed_back, mlp_gain_term = normalize_back(mixed, inverse_mlp, gain_mlp, normed_mlp_grad)
    mixed_grad = upstream + mixed_back
    pair_grad_attn = (gates_attn[:, :, None] * mixed_grad[:, None, :]).astype(jnp.bfloat16)
    gate_grad_attn = jnp.sum(pairs_attn * mixed_grad[:, None, :], axis=-1)
    sent_answer = dispatch(
        pair_grad_attn.reshape(length * TOP, model_width), places_attn, slot_count
    )
    answer_grad = trade(sent_answer.reshape(experts, capacity, model_width)).reshape(
        slot_count, model_width
    )
    out_term = contract_rows(attended, answer_grad)
    attended_grad = contract_cols(answer_grad, output_weight[0]).astype(jnp.bfloat16)
    attended_grad = attended_grad.reshape(experts, capacity, head_count, HEAD_DIM)
    attention = jnp.exp(masked_scores() - log_total)
    prob_grad = jnp.einsum(
        "schd,slhd->shcl", attended_grad, values_all, preferred_element_type=jnp.float32
    )
    row_delta = jnp.sum(attention * prob_grad, axis=-1, keepdims=True)
    score_grad = (attention * (prob_grad - row_delta)).astype(jnp.bfloat16)
    value_grad = jnp.einsum(
        "shcl,schd->slhd",
        attention.astype(jnp.bfloat16),
        attended_grad,
        preferred_element_type=jnp.float32,
    )
    key_grad = (
        jnp.einsum("shcl,schd->slhd", score_grad, queries, preferred_element_type=jnp.float32)
        * score_scale
    )
    query_grad = (
        jnp.einsum("shcl,slhd->schd", score_grad, keys_all, preferred_element_type=jnp.float32)
        * score_scale
    )
    query_grad = (
        rotate_back(query_grad, cos_slot, sin_slot)
        .reshape(slot_count, head_width)
        .astype(jnp.bfloat16)
    )
    query_term = contract_rows(arrived, query_grad)
    arrived_grad = contract_cols(query_grad, query_weight[0]).astype(jnp.bfloat16)
    query_part, out_part = (
        lax.psum_scatter(
            query_term.astype(jnp.bfloat16), "col", scatter_dimension=0, tiled=True
        ).astype(jnp.float32),
        lax.psum_scatter(
            out_term.astype(jnp.bfloat16), "col", scatter_dimension=0, tiled=True
        ).astype(jnp.float32),
    )
    key_sum, value_sum = (
        lax.psum_scatter(
            key_grad.reshape(experts * length, head_width).astype(jnp.bfloat16),
            "row",
            scatter_dimension=0,
            tiled=True,
        ).astype(jnp.float32),
        lax.psum_scatter(
            value_grad.reshape(experts * length, head_width).astype(jnp.bfloat16),
            "row",
            scatter_dimension=0,
            tiled=True,
        ).astype(jnp.float32),
    )
    back_attn = trade(arrived_grad.reshape(experts, capacity, model_width)).reshape(
        slot_count, model_width
    )
    normed_grad = jnp.sum(combine(back_attn, places_attn).astype(jnp.float32), axis=1)
    logit_grad_attn = gates_back(gates_attn, gate_grad_attn, own_attn, experts)
    normed_grad = normed_grad + jnp.dot(logit_grad_attn, router_attn.T, precision=precise)
    router_attn_term = jnp.dot(normed_low.astype(jnp.float32).T, logit_grad_attn, precision=precise)
    key_rows = rotate_back(key_sum.reshape(length, head_count, HEAD_DIM), cos_own, sin_own).reshape(
        length, head_width
    )
    projected_grad = jnp.concatenate([key_rows, value_sum], axis=1).astype(jnp.bfloat16)
    normed_grad = normed_grad + jnp.dot(
        projected_grad, kv_whole, preferred_element_type=jnp.float32
    )
    kv_term = lax.psum_scatter(
        contract_rows(projected_grad, normed_low), ("row", "col"), scatter_dimension=0, tiled=True
    )
    token_back, attn_gain_term = normalize_back(tokens, inverse_attn, gain_attn, normed_grad)
    input_grad = mixed_grad + token_back
    small_sums = lax.psum(
        (attn_gain_term, mlp_gain_term, router_attn_term, router_mlp_term), ("row", "col")
    )
    return (
        output,
        input_grad,
        small_sums[0],
        small_sums[1],
        small_sums[2],
        small_sums[3],
        kv_term,
        query_part[None],
        out_part[None],
        expert_term[None],
    )


def solution(mesh):
    in_specs = (
        P(("row", "col"), None),
        P(("row", "col"), None),
        P(),
        P(),
        P(),
        P(),
        P(("row", "col"), None),
        P("row", None, None),
        P("row", None, None),
        P("row", "col", None, None),
        P(None, "col", None),
        P(None, "col", None),
        P(None, "col"),
    )
    out_specs = (
        P(("row", "col"), None),
        P(("row", "col"), None),
        P(),
        P(),
        P(),
        P(),
        P(("row", "col"), None),
        P("row", "col", None),
        P("row", "col", None),
        P("row", "col", None, None),
    )
    return jax.shard_map(local, mesh=mesh, in_specs=in_specs, out_specs=out_specs, check_vma=False)
```

profile of v0, /device:TPU:0, one launch (start us, length us, event | category | flops | bytes accessed | tf_op | source)
XLA Modules:
  0.0 3981.4 jit_solution(6962483534922192512)
XLA Ops:
  11.8 116.4 %all-gather.6.cloned.1.call-done = bf16[4096,2048]{1,0:T(8,128)(2,1)} async-done(((bf16[128,2048]{1,0:T(8,128)(2,1)}), bf16[4096,2048]{1,0:T(8,128)(2,1)}) %all-gather.6.cloned.1.call-update) | async-done | bytes 16777232 | tf_op jit(solution)/shard_map/all_gather | solution.py:171
  128.2 11.4 fusion.111
  153.8 3.7 all-to-all-start
  157.8 12.3 copy.170
  170.4 4.8 reduce-window.20
  176.2 4.3 scatter_custom_fusion.4
  181.7 5.3 fusion.67
  187.9 4.3 copy.177
  204.8 4.1 all-to-all-start.1
  212.3 11.0 all-to-all-done.1
  231.6 3.8 scatter_custom_fusion.1
  244.7 3.6 mul.583
  251.9 4.3 scatter_custom_fusion.2
  258.4 4.5 all-to-all-start.4
  262.9 1232.2 %all-gather.12.cloned.1.call-done = bf16[1,5632,3,2048]{3,1,2,0:T(8,128)(2,1)} async-done(((bf16[1,704,3,2048]{3,1,2,0:T(8,128)(2,1)}), bf16[1,5632,3,2048]{3,1,2,0:T(8,128)(2,1)}) %all-gather.12.cloned.1.call-update) | async-done | bytes 69206032 | tf_op jit(solution)/shard_map/all_gather | solution.py:231
  1495.1 12.3 fusion.1
  1507.5 12.3 fusion.3
  1519.8 16.7 multiply_convert_fusion
  1536.5 12.8 fusion
  1549.4 11.9 fusion.13
  1564.8 12.3 fusion.14
  1579.2 4.3 all-to-all-start.3
  1591.7 6.3 all-to-all-done.3
  1604.9 6.5 multiply_reduce_fusion.2
  1611.8 3.9 reduce_sum.226
  1635.6 14.3 all-to-all-done.6
  1650.9 5.9 fusion.46
  1666.5 4.5 copy.166
  1674.5 3.9 convert_bitcast_fusion.3
  1678.5 3.5 copy.168
  1690.5 5.8 convolution_convert_fusion.1
  1697.9 5.7 convolution_convert_fusion
  1704.0 13.3 convert_bitcast_fusion
  1717.3 13.0 convert_bitcast_fusion.1
  1730.3 10.8 convert_bitcast_fusion.2
  1741.1 46.5 %pad_maximum_fusion = bf16[5632,3,2048]{2,0,1:T(8,128)(2,1)} fusion(bf16[5632,1,2048]{2,0,1:T(8,128)(2,1)} %convert_bitcast_fusion, bf16[5632,1,2048]{2,0,1:T(8,128)(2,1)} %convert_bitcast_fusion.1, bf16[5632,1,2048]{2,0,1:T(8,128)(2,1)} %convert_bitcast_fusion.2), kind=kLoop, calls=%fused_computation.11 | loop fusion | flops 69206016 | bytes 138412032 | tf_op jit(solution)/shard_map/stack | solution.py:257
  1790.5 6.8 fusion.15
  1797.2 4.4 all-to-all-start.7
  1803.8 12.4 all-to-all-done.7
  1823.3 5.1 reduce_sum.232
  1833.5 8.5 fusion.113
  1844.7 15.3 fusion.116
  1862.5 28.2 reduce-scatter.13.cloned.1.call-done
  1893.5 147.4 %reduce-scatter.15.cloned.1.call-done = bf16[256,2048]{1,0:T(8,128)(2,1)} async-done(((bf16[2048,2048]{1,0:T(8,128)(2,1)}), bf16[256,2048]{1,0:T(8,128)(2,1)}) %reduce-scatter.15.cloned.1.call-update) | async-done | bytes 1048592 | tf_op jit(solution)/shard_map/reduce_scatter | solution.py:326
  2043.7 1085.3 %reduce-scatter.17.cloned.1.call-done = bf16[704,3,2048]{2,0,1:T(8,128)(2,1)} async-done(((bf16[5632,3,2048]{2,0,1:T(8,128)(2,1)}), bf16[704,3,2048]{2,0,1:T(8,128)(2,1)}) %reduce-scatter.17.cloned.1.call-update) | async-done | bytes 8650768 | tf_op jit(solution)/shard_map/reduce_scatter | solution.py:256
  3129.0 12.0 bitcast_convert_fusion
  3141.0 117.7 %all-reduce.7.cloned.1.call-done = (f32[2048]{0:T(1024)}, f32[2048]{0:T(1024)}, f32[2048,4]{0,1:T(4,128)}, f32[2048,4]{0,1:T(4,128)}) async-done(((f32[2048]{0:T(1024)}, f32[2048]{0:T(1024)}, f32[2048,4]{0,1:T(4,128)}, f32[2048,4]{0,1:T(4,128)}), (f32[2048]{0:T(1024)}, f32[2048]{0:T(1024)}, f32[2048,4]{0,1:T(4,128)}, f32[2048,4]{0,1:T(4,128)})) %all-reduce.7.cloned.1.call-update) | async-done | bytes 81936 | tf_op jit(solution)/shard_map/psum | solution.py:363
  3258.7 710.6 %reduce-scatter.11.cloned.1.call-done = f32[128,2048]{1,0:T(8,128)} async-done(((f32[4096,2048]{1,0:T(8,128)}), f32[128,2048]{1,0:T(8,128)}) %reduce-scatter.11.cloned.1.call-update) | async-done | bytes 1048592 | tf_op jit(solution)/shard_map/reduce_scatter | solution.py:358
  (357 shorter events, 159.6 us)
Async XLA Ops:
  7.2 241.3 %copy-start = (bf16[2048,4]{0,1:T(4,128)(2,1)S(1)}, bf16[2048,4]{0,1:T(4,128)(2,1)}, u32[]{:S(2)}) copy-start(bf16[2048,4]{0,1:T(4,128)(2,1)} %param.20) | copy-start | bytes 49156
  7.2 121.0 %all-gather.6.cloned.1.call-start = ((), (), s32[]{:S(2)}) async-start(), calls=%async_computation.14 | async-start | bytes 17301504 | tf_op jit(solution)/shard_map/all_gather | solution.py:171
  7.9 180.0 %all-gather.8.cloned.1.call-start = ((), (), s32[]{:S(2)}) async-start(), calls=%async_computation.15 | async-start | bytes 2621440 | tf_op jit(solution)/shard_map/all_gather | solution.py:180
  11.7 197.1 %copy-start.4 = (bf16[128,2048]{1,0:T(8,128)(2,1)}, bf16[128,2048]{1,0:T(8,128)(2,1)S(1)}, u32[]{:S(2)}) copy-start(bf16[128,2048]{1,0:T(8,128)(2,1)S(1)} %fusion.51) | copy-start | bytes 1572868
  140.5 51.7 %all-gather.10.cloned.1.call-start = ((), (), s32[]{:S(2)}) async-start(), calls=%async_computation.16 | async-start | bytes 2621440 | tf_op jit(solution)/shard_map/all_gather | solution.py:179
  143.3 1351.8 %all-gather.12.cloned.1.call-start = ((), (), s32[]{:S(2)}) async-start(), calls=%async_computation.23 | async-start | bytes 77856768 | tf_op jit(solution)/shard_map/all_gather | solution.py:231
  145.0 35.6 copy-start.62
  150.3 61.5 %copy-start.68 = (s32[256,1]{0,1:T(1,128)}, s32[256,1]{0,1:T(1,128)S(1)}, u32[]{:S(2)}) copy-start(s32[256,1]{0,1:T(1,128)S(1)} %get-tuple-element.53) | copy-start | bytes 3076
  153.8 27.9 all-to-all-start
  157.7 18.1 copy-start.70
  157.7 18.2 copy-start.69
  157.7 23.2 copy-start.71
  187.9 6.7 copy-start.13
  187.9 6.7 copy-start.15
  192.2 9.3 slice-start
  204.8 18.4 all-to-all-start.1
  211.8 12.9 copy-start.64
  229.5 1386.1 %copy-start.10 = (f32[128,2048]{1,0:T(8,128)}, f32[128,2048]{1,0:T(8,128)S(1)}, u32[]{:S(2)}) copy-start(f32[128,2048]{1,0:T(8,128)S(1)} %get-tuple-element.22) | copy-start | bytes 3145732
  229.7 18.8 copy-start.23
  237.7 20.7 all-to-all-start.2
  258.4 1249.0 %copy-start.19 = (bf16[4,64,2048]{2,1,0:T(8,128)(2,1)}, bf16[4,64,2048]{2,1,0:T(8,128)(2,1)S(1)}, u32[]{:S(2)}) copy-start(bf16[4,64,2048]{2,1,0:T(8,128)(2,1)S(1)} %all-to-all-done.2) | copy-start | bytes 3145732
  258.4 1261.3 %all-to-all-start.4 = ((bf16[4,64,2048]{2,1,0:T(8,128)(2,1)}), bf16[4,64,2048]{2,1,0:T(8,128)(2,1)}, u32[]{:S(2)}, u32[]{:S(2)}) async-start(bf16[4,64,2048]{2,1,0:T(8,128)(2,1)} %bitcast.273), calls=%async_computation.4 | async-start | bytes 2097152 | tf_op jit(solution)/shard_map/all_to_all | solution.py:105
  1536.5 12.8 copy-start.32
  1536.5 12.8 copy-start.34
  1561.3 17.9 all-to-all-start.5
  1577.1 6.3 copy-start.30
  1579.2 18.8 all-to-all-start.3
  1604.9 6.8 copy-start.25
  1611.7 6.8 copy-start.60
  1629.7 5.9 copy-start.56
  1632.0 17.9 all-to-all-start.6
  1635.5 192.9 %reduce-scatter.7.cloned.1.call-start = ((), (), s32[]{:S(2)}) async-start(), calls=%async_computation.17 | async-start | bytes 2621440 | tf_op jit(solution)/shard_map/reduce_scatter | solution.py:331
  1650.9 6.2 copy-start.22
  1674.5 157.1 %reduce-scatter.9.cloned.1.call-start = ((), (), s32[]{:S(2)}) async-start(), calls=%async_computation.18 | async-start | bytes 2621440 | tf_op jit(solution)/shard_map/reduce_scatter | solution.py:337
  1683.9 206.8 %reduce-scatter.13.cloned.1.call-start = ((), (), s32[]{:S(2)}) async-start(), calls=%async_computation.20 | async-start | bytes 9437184 | tf_op jit(solution)/shard_map/reduce_scatter | solution.py:323
  1696.3 344.6 %reduce-scatter.15.cloned.1.call-start = ((), (), s32[]{:S(2)}) async-start(), calls=%async_computation.21 | async-start | bytes 9437184 | tf_op jit(solution)/shard_map/reduce_scatter | solution.py:326
  1703.6 13.7 copy-start.20
  1703.6 1425.4 %reduce-scatter.17.cloned.1.call-start = ((), (), s32[]{:S(2)}) async-start(), calls=%async_computation.22 | async-start | bytes 77856768 | tf_op jit(solution)/shard_map/reduce_scatter | solution.py:256
  1717.3 13.0 copy-start.33
  1797.2 18.9 all-to-all-start.7
  1801.7 1457.1 %all-reduce.7.cloned.1.call-start = ((), (), s32[]{:S(2)}) async-start(), calls=%async_computation.24 | async-start | bytes 163840 | tf_op jit(solution)/shard_map/psum | solution.py:363
  1833.5 8.6 copy-start.12
  1833.5 8.6 copy-start.36
  1833.5 8.6 copy-start.54
  1833.5 8.6 copy-start.58
  1833.5 8.6 copy-start.66
  1844.6 2124.7 %reduce-scatter.11.cloned.1.call-start = ((), (), s32[]{:S(2)}) async-start(), calls=%async_computation.19 | async-start | bytes 34603008 | tf_op jit(solution)/shard_map/reduce_scatter | solution.py:358
  3129.0 845.7 %copy-start.1 = (bf16[2048,4]{0,1:T(4,128)(2,1)S(1)}, bf16[2048,4]{0,1:T(4,128)(2,1)}, u32[]{:S(2)}) copy-start(bf16[2048,4]{0,1:T(4,128)(2,1)} %param.20) | copy-start | bytes 49156
  (45 other events, 124.4 us)
Sparse Core Ops, SparseCore 0:
  11.1 117.0 all-gather.5
  140.6 20.7 all-gather.7
  163.6 23.9 all-gather.9
  188.9 1306.1 all-gather.11
  1674.6 30.2 reduce-scatter.6
  1707.8 31.1 reduce-scatter.8
  1743.2 147.4 reduce-scatter.12
  1894.3 146.5 reduce-scatter.14
  2044.8 1084.0 reduce-scatter.16
  3135.5 123.1 all-reduce.6
  3261.6 707.6 reduce-scatter.10
where the time goes:
time: 3990 us; the launch traced here: 3980 us
  waiting for transfers between devices  3490 us (87%)
  matrix products  206 us (5%)
  local copies, waits for them, and re-layouts  123 us (3%)
  other arithmetic  119 us (3%)
    all_gather x1, waiting for transfers between devices, local(): gathered = lax.all_gather(local_weight, 'col', axis=0, tiled=True)  1230 us
    reduce_scatter x1, waiting for transfers between devices, local(): lax.psum_scatter(jnp.stack([contract_rows(gate_grad, arrived_mlp), contra...  1090 us
    reduce_scatter x1, waiting for transfers between devices, local(): lax.psum_scatter(contract_rows(projected_grad, normed_low), ('row', 'col'...  711 us
    reduce_scatter x1, waiting for transfers between devices, local(): lax.psum_scatter(out_term.astype(jnp.bfloat16), 'col', scatter_dimension=...  147 us
    psum x1, waiting for transfers between devices, local(): lax.psum((attn_gain_term, mlp_gain_term, router_attn_term, router_mlp_ter...  118 us
    all_gather x1, waiting for transfers between devices, local(): kv_whole = lax.all_gather(kv_weight, ('row', 'col'), axis=0, tiled=True)  116 us
  transfers between devices with their start and end apart: 19, of which 12 were waited for; matrix products, arithmetic and copies ran while one was open for 8% of the time, Pallas kernels for 0%

commit v1 on v0

v1 whole, which is shorter than its diff:
```python
import functools

import jax
import jax.numpy as jnp
from jax import lax
from jax.experimental import pallas as pl
from jax.experimental.pallas import tpu as pltpu
from jax.sharding import PartitionSpec as P

HEAD_DIM = 128
TOP = 2
BOTH = ("row", "col")

eps = 1e-06
theta = 10000.0
far_below = -1e30
F32 = jnp.float32
LOW = jnp.bfloat16


def dot(left, right, left_dim, right_dim):
    return lax.dot_general(
        left, right, (((left_dim,), (right_dim,)), ((), ())), preferred_element_type=F32
    )


def rope_tables(length):
    half_dim = HEAD_DIM // 2
    frequency = theta ** (-jnp.arange(half_dim, dtype=F32) / half_dim)
    angles = jnp.arange(length, dtype=F32)[:, None] * frequency
    cosine, sine = jnp.cos(angles), jnp.sin(angles)
    return (
        jnp.concatenate([cosine, cosine], axis=1),
        jnp.concatenate([-sine, sine], axis=1),
    )


def swap_halves(values):
    return pltpu.roll(values, HEAD_DIM // 2, 1)


def probabilities(query, key, allowed, scale):
    scores = jnp.where(allowed, dot(query, key, 1, 1) * scale, far_below)
    exponent = jnp.exp(scores - jnp.max(scores, axis=1, keepdims=True))
    return exponent / jnp.sum(exponent, axis=1, keepdims=True)


def allowed_keys(prefix, length):
    query_at = lax.broadcasted_iota(jnp.int32, (length, length), 0)
    key_at = lax.broadcasted_iota(jnp.int32, (length, length), 1)
    return (key_at <= query_at) | (key_at < prefix)


def attend_kernel(
    seqs, length, width, scale,
    prefix_ref, tok_ref, gain_ref, wkv_ref, wq_ref, cos_ref, sin_ref, sel_ref,
    normed_ref, q_ref, k_ref, v_ref, att_ref, slot_ref,
):
    first = pl.program_id(0) * seqs
    tokens = tok_ref[...].astype(F32)
    inverse = lax.rsqrt(jnp.mean(tokens * tokens, axis=1, keepdims=True) + eps)
    normed = (tokens * inverse * gain_ref[...]).astype(LOW)
    normed_ref[...] = normed
    kv = dot(normed, wkv_ref[...], 1, 1)
    qs = dot(normed, wq_ref[...], 1, 0)
    cosine, sine = cos_ref[...], sin_ref[...]
    v_ref[...] = kv[:, width:].astype(LOW)
    for s in range(seqs):
        rows = slice(s * length, (s + 1) * length)
        allowed = allowed_keys(prefix_ref[first + s], length)
        for h in range(width // HEAD_DIM):
            cols = slice(h * HEAD_DIM, (h + 1) * HEAD_DIM)
            key = kv[rows, cols]
            key = (key * cosine + swap_halves(key) * sine).astype(LOW)
            query = qs[rows, cols]
            query = (query * cosine + swap_halves(query) * sine).astype(LOW)
            k_ref[rows, cols] = key
            q_ref[rows, cols] = query
            probs = probabilities(query, key, allowed, scale).astype(LOW)
            att_ref[rows, cols] = dot(probs, v_ref[rows, cols], 1, 0).astype(LOW)
        slot_ref[s, 0] = dot(sel_ref[s], att_ref[rows, :], 1, 0).astype(LOW)


def attend_back_kernel(
    seqs, length, width, scale,
    prefix_ref, mg_ref, wo_ref, gate_ref, q_ref, k_ref, v_ref, att_ref, cos_ref, sin_ref, sel_ref,
    dq_ref, dkv_ref, attg_ref, slot_ref,
):
    first = pl.program_id(0) * seqs
    raw = dot(mg_ref[...], wo_ref[...], 1, 1)
    cosine, sine = cos_ref[...], sin_ref[...]
    for s in range(seqs):
        rows = slice(s * length, (s + 1) * length)
        allowed = allowed_keys(prefix_ref[first + s], length)
        gate = jnp.broadcast_to(gate_ref[s], (HEAD_DIM, length)).T
        for h in range(width // HEAD_DIM):
            cols = slice(h * HEAD_DIM, (h + 1) * HEAD_DIM)
            vcols = slice(width + h * HEAD_DIM, width + (h + 1) * HEAD_DIM)
            query, key, value = q_ref[rows, cols], k_ref[rows, cols], v_ref[rows, cols]
            probs = probabilities(query, key, allowed, scale)
            att_grad = (raw[rows, cols] * gate).astype(LOW)
            attg_ref[rows, cols] = (att_ref[rows, cols].astype(F32) * gate).astype(LOW)
            prob_grad = dot(att_grad, value, 1, 1)
            delta = jnp.sum(probs * prob_grad, axis=1, keepdims=True)
            score_grad = (probs * (prob_grad - delta)).astype(LOW)
            dq = dot(score_grad, key, 1, 0) * scale
            dq_ref[rows, cols] = (dq * cosine - swap_halves(dq) * sine).astype(LOW)
            dk = dot(score_grad, query, 0, 0) * scale
            dkv_ref[rows, cols] = (dk * cosine - swap_halves(dk) * sine).astype(LOW)
            dkv_ref[rows, vcols] = dot(probs.astype(LOW), att_grad, 0, 0).astype(LOW)
        slot_ref[s, 0] = dot(sel_ref[s], dq_ref[rows, :], 1, 0).astype(LOW)


def expert_kernel(
    seqs, length, capacity,
    nm_ref, up_ref, sel_ref, gate_ref, wg_ref, wu_ref, wd_ref,
    x_ref, u_ref, gg_ref, ug_ref, hg_ref, dx_ref, down_ref, part_ref,
):
    gates = []
    for s in range(seqs):
        rows = slice(s * length, (s + 1) * length)
        slots = slice(s * capacity, (s + 1) * capacity)
        sel = sel_ref[s]
        x_ref[slots, :] = dot(sel, nm_ref[rows, :], 1, 0).astype(LOW)
        u_ref[slots, :] = dot(sel, up_ref[rows, :], 1, 0).astype(LOW)
        gates.append(jnp.sum(sel.astype(F32) * gate_ref[s], axis=1, keepdims=True))
    gate = jnp.concatenate(gates, axis=0)
    x, u = x_ref[...], u_ref[...]
    pre = dot(x, wg_ref[...], 1, 1)
    up = dot(x, wu_ref[...], 1, 1)
    sig = 1.0 / (1.0 + jnp.exp(-pre))
    act = pre * sig
    hidden = (act * up).astype(LOW)
    raw = dot(u, wd_ref[...], 1, 1)
    wide = hidden.astype(F32)
    part = jnp.sum(wide * raw, axis=1, keepdims=True)
    part_ref[...] = jnp.broadcast_to(part, part_ref.shape)
    hg_ref[...] = (wide * gate).astype(LOW)
    grad = raw * gate
    gate_grad = (grad * up * sig * (1.0 + pre * (1.0 - sig))).astype(LOW)
    up_grad = (grad * act).astype(LOW)
    gg_ref[...] = gate_grad
    ug_ref[...] = up_grad
    dx = dot(gate_grad, wg_ref[...], 1, 0) + dot(up_grad, wu_ref[...], 1, 0)
    dx = dx.astype(LOW)
    down = dot(hidden, wd_ref[...], 1, 0).astype(LOW)
    for s in range(seqs):
        slots = slice(s * capacity, (s + 1) * capacity)
        dx_ref[s, 0] = dx[slots]
        down_ref[s, 0] = down[slots]


def const_spec(shape):
    return pl.BlockSpec(shape, lambda g, *_: (0,) * len(shape), pipeline_mode=pl.Buffered(1))


def row_spec(rows, cols):
    return pl.BlockSpec((rows, cols), lambda g, *_: (g, 0))


def lead_spec(count, *rest):
    return pl.BlockSpec((count,) + rest, lambda g, *_: (g,) + (0,) * len(rest))


def slot_spec(seqs, per_row, capacity, cols):
    return pl.BlockSpec(
        (seqs, 1, capacity, cols), lambda g, *_: (g % per_row, g // per_row, 0, 0)
    )


def trade(buffer, axis="row"):
    return lax.all_to_all(buffer, axis, split_axis=0, concat_axis=0, tiled=True)


def spread(values, axis, size):
    return trade(jnp.broadcast_to(values[None], (size,) + values.shape), axis)


def after(values, *others):
    return lax.optimization_barrier((values,) + others)[0]


def small_total(values, devices):
    pieces = trade(values.reshape(devices, -1), BOTH)
    piece = jnp.sum(pieces, axis=0)
    return spread(piece, BOTH, devices).reshape(-1)


def ranks(hit):
    length = hit.shape[-1]
    earlier = jnp.arange(length)[:, None] < jnp.arange(length)[None, :]
    flat = hit.reshape(-1, length).astype(LOW)
    return dot(flat, earlier.astype(LOW), 1, 0).reshape(hit.shape).astype(jnp.int32)


def selection(hit, capacity):
    slot = jnp.arange(capacity, dtype=jnp.int32)[:, None]
    return hit[..., None, :] & (ranks(hit)[..., None, :] == slot)


def routed_gates(normed_low, router, chosen):
    logits = jnp.dot(normed_low, router, preferred_element_type=F32)
    highest = jnp.max(jnp.where(chosen, logits, -jnp.inf), axis=1, keepdims=True)
    weights = jnp.where(chosen, jnp.exp(jnp.minimum(logits - highest, 0.0)), 0.0)
    return weights / jnp.sum(weights, axis=1, keepdims=True)


def outer_sum(weights, table):
    total = weights[:, 0:1] * table[:, 0][None, :]
    for e in range(1, weights.shape[1]):
        total = total + weights[:, e : e + 1] * table[:, e][None, :]
    return total


def router_term(normed_low, logit_grad):
    return jnp.dot(normed_low.astype(F32).T, logit_grad, precision=lax.Precision.HIGHEST)


def scattered(sel, rows):
    return jnp.stack([dot(sel[e], rows[e], 0, 0) for e in range(sel.shape[0])])


def local(
    inputs, cotangent, attn_gain, mlp_gain, attn_router, mlp_router, kv_weight, query_weight,
    output_weight, expert_weight, attn_routes, mlp_routes, prefix_len,
):
    length, model = inputs.shape
    n_row, n_col = lax.axis_size("row"), lax.axis_size("col")
    devices = n_row * n_col
    experts = n_row
    total = devices * length
    capacity = length * TOP // experts
    slots = n_row * capacity
    head_width = query_weight.shape[2]
    width = head_width // n_col
    hidden = expert_weight.shape[1]
    scale = HEAD_DIM ** (-0.5)
    own_row, own_col = lax.axis_index("row"), lax.axis_index("col")
    seqs = 4 if n_col % 4 == 0 else 1
    per_row = n_col // seqs
    steps = devices // seqs

    packed = jnp.concatenate(
        [attn_routes.reshape(-1), mlp_routes.reshape(-1), prefix_len.reshape(-1)]
    )
    packed = spread(packed, "col", n_col)
    span = n_row * length * TOP
    routes_a = packed[:, :span].reshape(n_col, n_row, length, TOP)
    routes_m = packed[:, span : 2 * span].reshape(n_col, n_row, length, TOP)
    prefixes = packed[:, 2 * span :].T.reshape(-1)
    routes_a = routes_a.transpose(1, 0, 2, 3).reshape(devices, length, TOP)
    routes_m = routes_m.transpose(1, 0, 2, 3).reshape(devices, length, TOP)
    sel_a = selection(jnp.any(routes_a == own_row, axis=-1), capacity).astype(LOW)
    sel_m = selection(jnp.any(routes_m == own_row, axis=-1), capacity).astype(LOW)

    def own_side(routes):
        own = lax.dynamic_index_in_dim(routes, own_row, 0, keepdims=False)
        each = jnp.arange(experts, dtype=jnp.int32)
        chosen = jnp.any(own[:, :, None] == each[None, None, :], axis=1)
        sel = selection(chosen.T, capacity)
        kept = jnp.any(sel, axis=1).T
        return chosen, sel, kept

    chosen_a, own_sel_a, kept_a = own_side(attn_routes)
    chosen_m, own_sel_m, kept_m = own_side(mlp_routes)
    own_sel_a_low, own_sel_m_low = own_sel_a.astype(LOW), own_sel_m.astype(LOW)

    half = n_row // 2
    route_kv = []
    for d in range(devices):
        at = d % (devices // 2)
        route_kv.append((d, (at % half + half * (2 * d // devices)) * n_col + at // half))
    back_kv = [(b, a) for a, b in route_kv]
    kv_block = lax.ppermute(kv_weight, BOTH, route_kv)
    kv_rows = spread(kv_block, "row", n_row).reshape(2 * width, model)
    wq = lax.dynamic_slice_in_dim(query_weight[0], own_col * width, width, 1)
    wo = lax.dynamic_slice_in_dim(output_weight[0], own_col * width, width, 0)

    tok_all = lax.all_gather(inputs, BOTH, axis=0, tiled=True)
    up_all = lax.all_gather(after(cotangent, tok_all), BOTH, axis=0, tiled=True)

    cosine, sine = rope_tables(length)
    gain_attn, gain_mlp = attn_gain.astype(F32), mlp_gain.astype(F32)
    rows = seqs * length
    token_out = jax.ShapeDtypeStruct((total, width), LOW)
    slot_out = jax.ShapeDtypeStruct((n_col, n_row, capacity, width), LOW)
    params = pltpu.CompilerParams(vmem_limit_bytes=60 * 2**20)
    normed_all, q_all, k_all, v_all, att_all, att_slots = pl.pallas_call(
        functools.partial(attend_kernel, seqs, length, width, scale),
        grid_spec=pltpu.PrefetchScalarGridSpec(
            num_scalar_prefetch=1,
            grid=(steps,),
            in_specs=[
                row_spec(rows, model),
                const_spec((1, model)),
                const_spec((2 * width, model)),
                const_spec((model, width)),
                const_spec((length, HEAD_DIM)),
                const_spec((length, HEAD_DIM)),
                lead_spec(seqs, capacity, length),
            ],
            out_specs=[row_spec(rows, model)]
            + [row_spec(rows, width)] * 4
            + [slot_spec(seqs, per_row, capacity, width)],
        ),
        out_shape=[jax.ShapeDtypeStruct((total, model), LOW)] + [token_out] * 4 + [slot_out],
        compiler_params=params,
        name="attend",
    )(prefixes, tok_all, gain_attn[None], kv_rows, wq, cosine, sine, sel_a)

    attended = trade(att_slots.reshape(n_col, slots, width), "col")
    attended = attended.transpose(1, 0, 2).reshape(slots, head_width)
    answers = dot(attended, output_weight[0], 1, 0).astype(LOW)
    returned = trade(answers.reshape(n_row, capacity, model))
    tokens = inputs.astype(F32)
    inverse_a = lax.rsqrt(jnp.mean(tokens * tokens, axis=-1, keepdims=True) + eps)
    normed_low = (tokens * inverse_a * gain_attn).astype(LOW)
    gates_a = routed_gates(normed_low, attn_router, chosen_a)
    kept_gates_a = jnp.where(kept_a, gates_a, 0.0)
    pairs_a = scattered(own_sel_a_low, returned)
    mixed = tokens + jnp.sum(kept_gates_a.T[:, :, None] * pairs_a, axis=0)
    inverse_m = lax.rsqrt(jnp.mean(mixed * mixed, axis=-1, keepdims=True) + eps)
    normed_m = (mixed * inverse_m * gain_mlp).astype(LOW)
    nm_all = lax.all_gather(after(normed_m, up_all), BOTH, axis=0, tiled=True)
    gates_m = routed_gates(normed_m, mlp_router, chosen_m)
    kept_gates_m = jnp.where(kept_m, gates_m, 0.0)
    gate_table = lax.all_gather(
        jnp.concatenate([kept_gates_a, kept_gates_m], axis=1).T, BOTH, axis=0
    )
    gate_a_all = lax.dynamic_index_in_dim(gate_table, own_row, 1)
    gate_m_all = lax.dynamic_index_in_dim(gate_table, experts + own_row, 1)

    block = expert_weight[0]
    slot_rows = seqs * capacity
    wide_slots = jax.ShapeDtypeStruct((devices * capacity, model), LOW)
    hidden_slots = jax.ShapeDtypeStruct((devices * capacity, hidden), LOW)
    grouped = jax.ShapeDtypeStruct((n_col, n_row, capacity, model), LOW)
    x, u, gg, ug, hg, dx, down, part = pl.pallas_call(
        functools.partial(expert_kernel, seqs, length, capacity),
        grid_spec=pltpu.PrefetchScalarGridSpec(
            num_scalar_prefetch=0,
            grid=(steps,),
            in_specs=[
                row_spec(rows, model),
                row_spec(rows, model),
                lead_spec(seqs, capacity, length),
                lead_spec(seqs, 1, length),
                const_spec((hidden, model)),
                const_spec((hidden, model)),
                const_spec((hidden, model)),
            ],
            out_specs=[row_spec(slot_rows, model)] * 2
            + [row_spec(slot_rows, hidden)] * 3
            + [slot_spec(seqs, per_row, capacity, model)] * 2
            + [row_spec(slot_rows, 128)],
        ),
        out_shape=[wide_slots] * 2
        + [hidden_slots] * 3
        + [grouped] * 2
        + [jax.ShapeDtypeStruct((devices * capacity, 128), F32)],
        compiler_params=params,
        name="experts",
    )(nm_all, up_all, sel_m, gate_m_all, block[:, 0], block[:, 1], block[:, 2])
    dx_sum = lax.psum_scatter(
        dx.reshape(-1, model), "col", scatter_dimension=0, tiled=True
    )
    back_m = trade(dx_sum.reshape(n_row, capacity, model))
    parts = trade(part[:, 0].reshape(devices, capacity), BOTH)
    parts = jnp.sum(parts.reshape(experts, n_col, capacity), axis=1)
    gate_grad_m = jnp.sum(jnp.where(own_sel_m, parts[:, :, None], 0.0), axis=1).T

    def logit_grads(gates, grads):
        return gates * (grads - jnp.sum(gates * grads, axis=1, keepdims=True))

    logit_m = logit_grads(gates_m, gate_grad_m)
    normed_m_grad = jnp.sum(scattered(own_sel_m_low, back_m), axis=0)
    normed_m_grad = normed_m_grad + outer_sum(logit_m, mlp_router.astype(F32))
    upstream = cotangent.astype(F32)
    scaled = normed_m_grad * gain_mlp
    inner = jnp.mean(scaled * mixed, axis=-1, keepdims=True)
    mixed_grad = upstream + inverse_m * scaled - mixed * inverse_m * inverse_m * inverse_m * inner
    mg_all = lax.all_gather(mixed_grad.astype(LOW), BOTH, axis=0, tiled=True)

    down_sum = lax.psum_scatter(
        after(down.reshape(-1, model), mg_all), "col", scatter_dimension=0, tiled=True
    )
    back_down = trade(down_sum.reshape(n_row, capacity, model))
    pairs_m = scattered(own_sel_m_low, back_down)
    output = (mixed + jnp.sum(kept_gates_m.T[:, :, None] * pairs_m, axis=0)).astype(LOW)
    expert_grad = jnp.stack([dot(gg, x, 0, 0), dot(ug, x, 0, 0), dot(hg, u, 0, 0)], axis=1)
    mlp_gain_term = jnp.sum(normed_m_grad * mixed * inverse_m, axis=0)
    gate_grad_a = jnp.sum(pairs_a * mixed_grad[None], axis=-1).T
    logit_a = logit_grads(gates_a, gate_grad_a)
    early = small_total(
        jnp.concatenate(
            [
                mlp_gain_term,
                router_term(normed_m, logit_m).reshape(-1),
                router_term(normed_low, logit_a).reshape(-1),
            ]
        ),
        devices,
    )

    dq_all, dkv, attg, dq_slots = pl.pallas_call(
        functools.partial(attend_back_kernel, seqs, length, width, scale),
        grid_spec=pltpu.PrefetchScalarGridSpec(
            num_scalar_prefetch=1,
            grid=(steps,),
            in_specs=[
                row_spec(rows, model),
                const_spec((width, model)),
                lead_spec(seqs, 1, length),
            ]
            + [row_spec(rows, width)] * 4
            + [
                const_spec((length, HEAD_DIM)),
                const_spec((length, HEAD_DIM)),
                lead_spec(seqs, capacity, length),
            ],
            out_specs=[
                row_spec(rows, width),
                row_spec(rows, 2 * width),
                row_spec(rows, width),
                slot_spec(seqs, per_row, capacity, width),
            ],
        ),
        out_shape=[
            token_out,
            jax.ShapeDtypeStruct((total, 2 * width), LOW),
            token_out,
            slot_out,
        ],
        compiler_params=params,
        name="attend_back",
    )(prefixes, mg_all, wo, gate_a_all, q_all, k_all, v_all, att_all, cosine, sine, sel_a)

    piece = 2 * width // n_row
    dkv = trade(dkv.reshape(total, n_row, piece).transpose(1, 0, 2))
    projected_grad = jnp.sum(dkv.astype(F32), axis=0).astype(LOW)
    dq_own = trade(dq_slots.reshape(n_col, slots, width), "col")
    dq_own = dq_own.transpose(1, 0, 2).reshape(slots, head_width)
    arrived_grad = dot(dq_own, query_weight[0], 1, 1).astype(LOW)
    back_a = trade(arrived_grad.reshape(n_row, capacity, model))
    own_grad = trade(projected_grad.reshape(devices, length, piece), BOTH)
    own_grad = own_grad.transpose(1, 0, 2).reshape(length, 2 * head_width)
    kv_whole = lax.all_gather(after(kv_block, up_all), BOTH, axis=0, tiled=True)
    normed_grad = jnp.sum(scattered(own_sel_a_low, back_a), axis=0)
    normed_grad = normed_grad + dot(own_grad, kv_whole, 1, 0)
    normed_grad = normed_grad + outer_sum(logit_a, attn_router.astype(F32))
    scaled_a = normed_grad * gain_attn
    inner_a = jnp.mean(scaled_a * tokens, axis=-1, keepdims=True)
    input_grad = (
        mixed_grad + inverse_a * scaled_a - tokens * inverse_a * inverse_a * inverse_a * inner_a
    )
    attn_gain_term = jnp.sum(normed_grad * tokens * inverse_a, axis=0)
    attn_gain_grad = jnp.sum(lax.all_gather(attn_gain_term, BOTH, axis=0), axis=0)

    kv_grad = lax.ppermute(dot(projected_grad, normed_all, 0, 0), BOTH, back_kv)
    out_grad = dot(attg, mg_all, 0, 0)
    query_grad = trade(
        dot(normed_all, dq_all, 0, 0).astype(LOW).reshape(n_col, model // n_col, width), "col"
    )
    query_grad = query_grad.transpose(1, 0, 2).reshape(model // n_col, head_width).astype(F32)
    router_size = model * experts
    return (
        output,
        input_grad,
        attn_gain_grad,
        early[:model],
        early[model + router_size :].reshape(model, experts),
        early[model : model + router_size].reshape(model, experts),
        kv_grad,
        query_grad[None],
        out_grad[None],
        expert_grad[None],
    )


def solution(mesh):
    in_specs = (
        P(("row", "col"), None),
        P(("row", "col"), None),
        P(),
        P(),
        P(),
        P(),
        P(("row", "col"), None),
        P("row", None, None),
        P("row", None, None),
        P("row", "col", None, None),
        P(None, "col", None),
        P(None, "col", None),
        P(None, "col"),
    )
    out_specs = (
        P(("row", "col"), None),
        P(("row", "col"), None),
        P(),
        P(),
        P(),
        P(),
        P(("row", "col"), None),
        P("row", "col", None),
        P("row", "col", None),
        P("row", "col", None, None),
    )
    return jax.shard_map(local, mesh=mesh, in_specs=in_specs, out_specs=out_specs, check_vma=False)
```

time: 3990 us -> 1240 us (0.31)
  waiting for transfers between devices: 3490 us -> 624 us
  Pallas kernels: 0 us -> 156 us
  blocking collectives: 0 us -> 139 us
  matrix products: 206 us -> 116 us
  other arithmetic: 119 us -> 36.9 us
  local copies, waits for them, and re-layouts: 123 us -> 54.2 us
  starting transfers between devices: 32.5 us -> 86.8 us
    reduce_scatter x6 -> x2, waiting for transfers between devices: 1970 us -> 135 us  [the longest x1 135 us: local(): lax.psum_scatter(dx.reshape(-1, model), 'col', scatter_dimension=0, tiled...]
    all_gather x4 -> x5, waiting for transfers between devices: 1350 us -> 262 us  [the longest x1 120 us: local(): tok_all = lax.all_gather(inputs, BOTH, axis=0, tiled=True)]
    all_to_all x8 -> x14, waiting for transfers between devices: 46 us -> 226 us  [trade(): return lax.all_to_all(buffer, axis, split_axis=0, concat_axis=0, tiled=True)]
    pallas_call x0 -> x3, Pallas kernels: none -> 156 us  [the longest x1 56.4 us: local(): pl.pallas_call(functools.partial(expert_kernel, seqs, length, capacity),...]
    all_gather x0 -> x2, blocking collectives: none -> 139 us  [the longest x1 70.4 us: local(): lax.all_gather(attn_gain_term, BOTH, axis=0)]
    psum x1 -> x0, waiting for transfers between devices: 118 us -> none  [local(): lax.psum((attn_gain_term, mlp_gain_term, router_attn_term, router_mlp_ter...]
    dot_general x30 -> x33, matrix products: 206 us -> 116 us  [the longest x29 112 us: dot(): lax.dot_general(left, right, (((left_dim,), (right_dim,)), ((), ())), pre...]
    another operation x12 -> x0, other arithmetic: 56.7 us -> none  [the longest x1 46.5 us: local(): jnp.stack([contract_rows(gate_grad, arrived_mlp), contract_rows(up_grad,...]
  transfers between devices with their start and end apart: 19 -> 23, of which waited for: 12 -> 15; matrix products, arithmetic and copies ran while one was open for 8% -> 15% of each run, Pallas kernels for 0% -> 8%
where the time goes in v1:
time: 1240 us; the launch traced here: 1230 us
  waiting for transfers between devices  624 us (50%)
  Pallas kernels  156 us (13%)
  blocking collectives  139 us (11%)
  matrix products  116 us (9%)
  starting transfers between devices  86.8 us (7%)
  local copies, waits for them, and re-layouts  54.2 us (4%)
  other arithmetic  36.9 us (3%)
  between operations  15.3 us (1%)
    all_to_all x14, waiting for transfers between devices, trade(): return lax.all_to_all(buffer, axis, split_axis=0, concat_axis=0, tiled=True)  226 us
    reduce_scatter x1, waiting for transfers between devices, local(): lax.psum_scatter(dx.reshape(-1, model), 'col', scatter_dimension=0, tiled...  135 us
    all_gather x1, waiting for transfers between devices, local(): tok_all = lax.all_gather(inputs, BOTH, axis=0, tiled=True)  120 us
    dot_general x29, matrix products, dot(): lax.dot_general(left, right, (((left_dim,), (right_dim,)), ((), ())), pre...  112 us
    all_gather x1, waiting for transfers between devices, local(): mg_all = lax.all_gather(mixed_grad.astype(LOW), BOTH, axis=0, tiled=True)  112 us
    all_to_all x14, starting transfers between devices, trade(): return lax.all_to_all(buffer, axis, split_axis=0, concat_axis=0, tiled=True)  82.3 us
    all_gather x1, blocking collectives, local(): lax.all_gather(attn_gain_term, BOTH, axis=0)  70.4 us
    all_gather x1, blocking collectives, local(): lax.all_gather(jnp.concatenate([kept_gates_a, kept_gates_m], axis=1).T, B...  68.5 us
  transfers between devices with their start and end apart: 23, of which 15 were waited for; matrix products, arithmetic and copies ran while one was open for 15% of the time, Pallas kernels for 8%

profile of v1, /device:TPU:0, one launch (start us, length us, event | category | flops | bytes accessed | tf_op | source)
XLA Modules:
  0.0 1228.7 jit_solution(5275888186069904577)
XLA Ops:
  8.0 120.2 %all-gather.8.cloned.1.call-done.tok_ref = bf16[4096,2048]{1,0:T(8,128)(2,1)} async-done(((bf16[128,2048]{1,0:T(8,128)(2,1)}), bf16[4096,2048]{1,0:T(8,128)(2,1)}) %all-gather.8.cloned.1.call-update) | async-done | bytes 16777232 | tf_op jit(solution)/shard_map/all_gather | solution.py:279
  133.2 5.4 all-to-all-start
  139.9 18.4 %all-to-all-done = s32[8,1,2052]{2,1,0:T(1,128)S(1)} async-done(((s32[8,1,2052]{2,1,0:T(1,128)}), s32[8,1,2052]{2,1,0:T(1,128)S(1)}, u32[]{:S(2)}, u32[]{:S(2)}) %all-to-all-start) | async-done | bytes 65696 | tf_op jit(solution)/shard_map/all_to_all | solution.py:172
  159.9 3.6 all-to-all-start.1
  170.3 30.8 %all-to-all-done.1 = bf16[4,128,2048]{2,1,0:T(8,128)(2,1)S(1)} async-done(((bf16[4,128,2048]{2,1,0:T(8,128)(2,1)}), bf16[4,128,2048]{2,1,0:T(8,128)(2,1)S(1)}, u32[]{:S(2)}, u32[]{:S(2)}) %all-to-all-start.1) | async-done | bytes 2097184 | tf_op jit(solution)/shard_map/all_to_all | solution.py:172
  202.4 51.2 %attend.1 = (bf16[4096,2048]{1,0:T(8,128)(2,1)}, bf16[4096,256]{1,0:T(8,128)(2,1)}, bf16[4096,256]{1,0:T(8,128)(2,1)}, bf16[4096,256]{1,0:T(8,128)(2,1)}, bf16[4...) custom-call(s32[32]{0:T(128)} %reshape.217.prefix_ref, bf16[4096,2048]{1,0:T(8,128)(2,1)} %all-gather.8.cloned.1.call-done.tok_ref, ...), custom_call_target="tpu_custom_call" | custom-call | tf_op jit(solution)/shard_map/attend/pallas_call | solution.py:288
  255.9 5.4 all-to-all-start.2
  262.3 25.1 %all-to-all-done.2 = bf16[8,256,256]{1,2,0:T(8,128)(2,1)S(1)} async-done(((bf16[8,256,256]{1,2,0:T(8,128)(2,1)}), bf16[8,256,256]{1,2,0:T(8,128)(2,1)S(1)}, u32[]{:S(2)}, u32[]{:S(2)}) %all-to-all-start.2) | async-done | bytes 1048608 | tf_op jit(solution)/shard_map/all_to_all | solution.py:172
  287.4 6.7 fusion.5
  294.2 3.5 all-to-all-start.3
  298.4 13.7 %all-to-all-done.3 = bf16[4,64,2048]{2,1,0:T(8,128)(2,1)S(1)} async-done(((bf16[4,64,2048]{2,1,0:T(8,128)(2,1)}), bf16[4,64,2048]{2,1,0:T(8,128)(2,1)S(1)}, u32[]{:S(2)}, u32[]{:S(2)}) %all-to-all-start.3) | async-done | bytes 1048608 | tf_op jit(solution)/shard_map/all_to_all | solution.py:172
  321.9 6.1 slice_bitcast_fusion
  333.6 68.5 %all-gather = f32[256,128]{1,0:T(8,128)S(1)} all-gather(f32[8,128]{1,0:T(8,128)S(1)} %maximum_bitcast_fusion.1), channel_id=2, replica_groups=mesh['row'=4,'col'=8] {'row','col'}, dimensions={0}, use_global_device_ids=true | all-gather | bytes 135168 | tf_op jit(solution)/shard_map/all_gather | solution.py:327
  402.7 30.4 %all-gather.12.cloned.1.call-done.nm_ref = bf16[4096,2048]{1,0:T(8,128)(2,1)} async-done(((bf16[128,2048]{1,0:T(8,128)(2,1)}), bf16[4096,2048]{1,0:T(8,128)(2,1)}) %all-gather.12.cloned.1.call-update) | async-done | bytes 16777232 | tf_op jit(solution)/shard_map/all_gather | solution.py:324
  433.1 56.4 %experts.1 = (bf16[2048,2048]{1,0:T(8,128)(2,1)}, bf16[2048,2048]{1,0:T(8,128)(2,1)}, bf16[2048,704]{1,0:T(8,128)(2,1)}, bf16[2048,704]{1,0:T(8,128)(2,1)}, bf16...) custom-call(bf16[4096,2048]{1,0:T(8,128)(2,1)} %all-gather.12.cloned, ...), custom_call_target="tpu_custom_call" | custom-call | tf_op jit(solution)/shard_map/experts/pallas_call | solution.py:338
  491.8 2.8 all-to-all-start.5
  494.7 7.1 all-to-all-done.5
  501.7 135.0 %reduce-scatter.3.cloned.1.call-done = bf16[256,2048]{1,0:T(8,128)(2,1)} async-done(((bf16[2048,2048]{1,0:T(8,128)(2,1)}), bf16[256,2048]{1,0:T(8,128)(2,1)}) %reduce-scatter.3.cloned.1.call-update) | async-done | bytes 1048592 | tf_op jit(solution)/shard_map/reduce_scatter | solution.py:364
  636.8 4.3 all-to-all-start.4
  641.3 14.2 %all-to-all-done.4 = bf16[4,64,2048]{2,1,0:T(8,128)(2,1)} async-done(((bf16[4,64,2048]{2,1,0:T(8,128)(2,1)}), bf16[4,64,2048]{2,1,0:T(8,128)(2,1)}, u32[]{:S(2)}, u32[]{:S(2)}) %all-to-all-start.4) | async-done | bytes 1048608 | tf_op jit(solution)/shard_map/all_to_all | solution.py:172
  663.9 111.7 %all-gather.14.cloned.1.call-done.mg_ref = bf16[4096,2048]{1,0:T(8,128)(2,1)} async-done(((bf16[128,2048]{1,0:T(8,128)(2,1)}), bf16[4096,2048]{1,0:T(8,128)(2,1)}) %all-gather.14.cloned.1.call-update) | async-done | bytes 16777232 | tf_op jit(solution)/shard_map/all_gather | solution.py:382
  783.9 2.8 all-to-all-start.11
  789.0 7.1 all-to-all-done.11
  799.4 49.0 %attend_back.1 = (bf16[4096,256]{1,0:T(8,128)(2,1)}, bf16[4096,512]{1,0:T(8,128)(2,1)}, bf16[4096,256]{1,0:T(8,128)(2,1)}, bf16[8,4,64,256]{3,2,1,0:T(8,128)(2,1)}) custom-call(s32[32]{0:T(128)} %reshape.217.prefix_ref, bf16[4096,2048]{1,0:T(8,128)(2,1)} %all-gather.14.cloned.1.call-done.mg_ref, bf16[256,2048]{1,0:T(8,128)(2,1)} %dynamic-slice_bitcast_fusion.wo_ref, ...), custom_call_target="tpu_custom_call" | custom-call | tf_op jit(solution)/shard_map/attend_back/pallas_call | solution.py:405
  848.4 12.4 %convolution_convert_fusion = bf16[2048,256]{1,0:T(8,128)(2,1)} fusion(bf16[4096,2048]{1,0:T(8,128)(2,1)} %get-tuple-element.46, bf16[4096,256]{1,0:T(8,128)(2,1)} %get-tuple-element.47), kind=kOutput, calls=%fused_computation.18 | convolution fusion | flops 4295491584 | bytes 19922944 | tf_op jit(solution)/shard_map/dot_general | solution.py:22
  860.8 6.0 all-to-all-start.13
  866.9 11.3 convolution_bitcast_fusion.2
  880.5 30.3 %all-to-all-done.13 = bf16[8,256,256]{2,1,0:T(8,128)(2,1)S(1)} async-done(((bf16[8,256,256]{2,1,0:T(8,128)(2,1)}), bf16[8,256,256]{2,1,0:T(8,128)(2,1)S(1)}, u32[]{:S(2)}, u32[]{:S(2)}) %all-to-all-start.13) | async-done | bytes 1048608 | tf_op jit(solution)/shard_map/all_to_all | solution.py:172
  910.8 4.2 all-to-all-start.7
  915.0 11.3 convolution_bitcast_fusion.1
  926.3 2.7 bitcast_bitcast_fusion
  929.1 32.9 %all-to-all-done.7 = bf16[8,256,256]{1,2,0:T(8,128)(2,1)} async-done(((bf16[8,256,256]{1,2,0:T(8,128)(2,1)}), bf16[8,256,256]{1,2,0:T(8,128)(2,1)}, u32[]{:S(2)}, u32[]{:S(2)}) %all-to-all-start.7) | async-done | bytes 1048608 | tf_op jit(solution)/shard_map/all_to_all | solution.py:172
  962.0 5.1 all-to-all-start.9
  967.1 9.8 convolution_bitcast_fusion
  976.9 11.2 maximum_bitcast_fusion
  991.1 3.0 fusion.55
  999.0 7.1 fusion.8
  1006.1 9.2 all-to-all-done.9
  1015.3 4.5 all-to-all-start.8
  1019.8 12.8 %convolution_bitcast_fusion.3 = f32[1,256,2048]{2,1,0:T(8,128)} fusion(bf16[4096,256]{1,0:T(8,128)(2,1)} %get-tuple-element.48, bf16[4096,2048]{1,0:T(8,128)(2,1)} %all-gather.14.cloned.1.call-done.mg_ref), kind=kOutput, calls=%fused_computation.17 | convolution fusion | flops 4294967296 | bytes 20971520 | tf_op jit(solution)/shard_map/dot_general | solution.py:22
  1035.3 2.7 reshape.237
  1038.1 4.1 reduce_sum.207
  1042.1 6.1 all-to-all-start.10
  1048.3 8.5 fusion.59
  1064.9 36.7 %all-to-all-done.10 = bf16[32,128,128]{2,1,0:T(8,128)(2,1)S(1)} async-done(((bf16[32,128,128]{2,1,0:T(8,128)(2,1)}), bf16[32,128,128]{2,1,0:T(8,128)(2,1)S(1)}, u32[]{:S(2)}, u32[]{:S(2)}) %all-to-all-start.10) | async-done | bytes 1048608 | tf_op jit(solution)/shard_map/all_to_all | solution.py:172
  1102.9 10.2 fusion.22
  1113.1 25.8 %all-to-all-start.6 = ((bf16[4,64,2048]{2,1,0:T(8,128)(2,1)}), bf16[4,64,2048]{2,1,0:T(8,128)(2,1)}, u32[]{:S(2)}, u32[]{:S(2)}) async-start(bf16[4,64,2048]{2,1,0:T(8,128)(2,1)} %bitcast.274), calls=%async_computation.8 | async-start | bytes 2097152 | tf_op jit(solution)/shard_map/all_to_all | solution.py:172
  1138.9 70.4 %all-gather.1 = f32[65536]{0:T(1024)S(1)} all-gather(f32[2048]{0:T(1024)S(1)} %get-tuple-element.116), channel_id=3, replica_groups=mesh['row'=4,'col'=8] {'row','col'}, dimensions={0}, use_global_device_ids=true | all-gather | bytes 270336 | tf_op jit(solution)/shard_map/all_gather | solution.py:457
  (194 shorter events, 95.5 us)
Async XLA Ops:
  7.2 121.0 %all-gather.8.cloned.1.call-start = ((), (), s32[]{:S(2)}) async-start(), calls=%async_computation.16 | async-start | bytes 17301504 | tf_op jit(solution)/shard_map/all_gather | solution.py:279
  7.9 311.8 %all-gather.10.cloned.1.call-start = ((), (), s32[]{:S(2)}) async-start(), calls=%async_computation.17 | async-start | bytes 17301504 | tf_op jit(solution)/shard_map/all_gather | solution.py:280
  128.2 30.2 %collective-permute-start = (bf16[128,2048]{1,0:T(8,128)(2,1)}, bf16[128,2048]{1,0:T(8,128)(2,1)S(1)}, u32[]{:S(2)}, u32[]{:S(2)}) collective-permute-start(bf16[128,2048]{1,0:T(8,128)(2,1)} %param.19), channel_id=1, source_target_pairs={{0,0},{1,8},{2,1},{3,9},{4,2},{5,10},{6,3},{7,11},{8,4},{9,12},{10... | collective-permute-start | bytes 1572872 | tf_op jit(solution)/shard_map/ppermute | solution.py:274
  133.2 25.1 %all-to-all-start = ((s32[8,1,2052]{2,1,0:T(1,128)}), s32[8,1,2052]{2,1,0:T(1,128)S(1)}, u32[]{:S(2)}, u32[]{:S(2)}) async-start(s32[8,1,2052]{2,1,0:T(1,128)} %broadcast_in_dim.29), calls=%async_computation | async-start | bytes 139264 | tf_op jit(solution)/shard_map/all_to_all | solution.py:172
  158.3 1.6 copy-start.10
  159.9 41.2 %all-to-all-start.1 = ((bf16[4,128,2048]{2,1,0:T(8,128)(2,1)}), bf16[4,128,2048]{2,1,0:T(8,128)(2,1)S(1)}, u32[]{:S(2)}, u32[]{:S(2)}) async-start(bf16[4,128,2048]{2,1,0:T(8,128)(2,1)} %broadcast_in_dim.31), calls=%async_computation.1 | async-start | bytes 4194304 | tf_op jit(solution)/shard_map/all_to_all | solution.py:172
  253.6 8.5 copy-start
  255.9 31.5 %all-to-all-start.2 = ((bf16[8,256,256]{1,2,0:T(8,128)(2,1)}), bf16[8,256,256]{1,2,0:T(8,128)(2,1)S(1)}, u32[]{:S(2)}, u32[]{:S(2)}) async-start(bf16[8,256,256]{1,2,0:T(8,128)(2,1)} %copy.105), calls=%async_computation.2 | async-start | bytes 2097152 | tf_op jit(solution)/shard_map/all_to_all | solution.py:172
  262.3 35.4 %copy-start.23 = (f32[128]{0:T(128)}, f32[128]{0:T(128)S(1)}, u32[]{:S(2)}) copy-start(f32[128]{0:T(128)S(1)} %add_rsqrt_fusion.1) | copy-start | bytes 1540
  287.4 10.3 copy-start.14
  287.4 10.3 copy-start.16
  287.4 10.7 copy-start.26
  294.2 17.9 %all-to-all-start.3 = ((bf16[4,64,2048]{2,1,0:T(8,128)(2,1)}), bf16[4,64,2048]{2,1,0:T(8,128)(2,1)S(1)}, u32[]{:S(2)}, u32[]{:S(2)}) async-start(bf16[4,64,2048]{2,1,0:T(8,128)(2,1)} %bitcast.15), calls=%async_computation.3 | async-start | bytes 2097152 | tf_op jit(solution)/shard_map/all_to_all | solution.py:172
  297.7 135.4 %all-gather.12.cloned.1.call-start = ((), (), s32[]{:S(2)}) async-start(), calls=%async_computation.18 | async-start | bytes 17301504 | tf_op jit(solution)/shard_map/all_gather | solution.py:324
  298.3 23.5 %copy-start.11 = (pred[4,64,128]{2,1,0:T(32,128)(4,1)}, pred[4,64,128]{2,1,0:T(32,128)(4,1)S(1)}, u32[]{:S(2)}) copy-start(pred[4,64,128]{2,1,0:T(32,128)(4,1)S(1)} %get-tuple-element.146) | copy-start | bytes 98308
  314.7 3.0 copy-start.1
  316.2 2.2 copy-start.2
  319.7 317.1 %reduce-scatter.3.cloned.1.call-start = ((), (), s32[]{:S(2)}) async-start(), calls=%async_computation.19 | async-start | bytes 9437184 | tf_op jit(solution)/shard_map/reduce_scatter | solution.py:364
  320.0 8.0 copy-start.19
  320.1 7.9 copy-start.21
  321.9 8.8 copy-start.5
  489.5 5.1 copy-start.15
  489.5 151.6 %copy-start.20 = (pred[128,4]{0,1:T(4,128)(4,1)S(1)}, pred[128,4]{0,1:T(4,128)(4,1)}, u32[]{:S(2)}) copy-start(pred[128,4]{0,1:T(4,128)(4,1)} %copy-done.19) | copy-start | bytes 1540
  489.5 151.6 %copy-start.22 = (s32[4,128]{1,0:T(4,128)S(1)}, s32[4,128]{1,0:T(4,128)}, u32[]{:S(2)}) copy-start(s32[4,128]{1,0:T(4,128)} %copy-done.21) | copy-start | bytes 6148
  489.5 166.0 %copy-start.13 = (pred[4,64,128]{2,1,0:T(32,128)(4,1)S(1)}, pred[4,64,128]{2,1,0:T(32,128)(4,1)}, u32[]{:S(2)}) copy-start(pred[4,64,128]{2,1,0:T(32,128)(4,1)} %get-tuple-element.143) | copy-start | bytes 98308
  491.1 168.4 %copy-start.28 = (f32[128]{0:T(128)S(1)}, f32[128]{0:T(128)}, u32[]{:S(2)}) copy-start(f32[128]{0:T(128)} %copy-done.27) | copy-start | bytes 1540
  491.8 9.9 all-to-all-start.5
  636.8 18.8 %all-to-all-start.4 = ((bf16[4,64,2048]{2,1,0:T(8,128)(2,1)}), bf16[4,64,2048]{2,1,0:T(8,128)(2,1)}, u32[]{:S(2)}, u32[]{:S(2)}) async-start(bf16[4,64,2048]{2,1,0:T(8,128)(2,1)} %bitcast.275), calls=%async_computation.5 | async-start | bytes 2097152 | tf_op jit(solution)/shard_map/all_to_all | solution.py:172
  641.0 134.6 %all-gather.14.cloned.1.call-start = ((), (), s32[]{:S(2)}) async-start(), calls=%async_computation.20 | async-start | bytes 17301504 | tf_op jit(solution)/shard_map/all_gather | solution.py:382
  656.8 4.5 copy-start.9
  662.9 440.0 %all-gather.16.cloned.1.call-start = ((), (), s32[]{:S(2)}) async-start(), calls=%async_computation.22 | async-start | bytes 17301504 | tf_op jit(solution)/shard_map/all_gather | solution.py:447
  663.5 449.6 %reduce-scatter.5.cloned.1.call-start = ((), (), s32[]{:S(2)}) async-start(), calls=%async_computation.21 | async-start | bytes 9437184 | tf_op jit(solution)/shard_map/reduce_scatter | solution.py:384
  775.6 6.1 copy-start.18
  775.6 6.1 copy-start.24
  783.9 12.2 all-to-all-start.11
  796.9 64.0 %all-to-all-start.12 = ((f32[32,1,576]{2,1,0:T(1,128)}), f32[32,1,576]{2,1,0:T(1,128)S(1)}, u32[]{:S(2)}, u32[]{:S(2)}) async-start(f32[32,1,576]{2,1,0:T(1,128)} %broadcast_in_dim.35), calls=%async_computation.14 | async-start | bytes 163840 | tf_op jit(solution)/shard_map/all_to_all | solution.py:172
  848.4 18.5 %copy-start.17 = (bf16[2048,4]{0,1:T(4,128)(2,1)S(1)}, bf16[2048,4]{0,1:T(4,128)(2,1)}, u32[]{:S(2)}) copy-start(bf16[2048,4]{0,1:T(4,128)(2,1)} %param.17) | copy-start | bytes 49156
  848.4 18.5 %copy-start.25 = (pred[4,128]{1,0:T(4,128)(4,1)S(1)}, pred[4,128]{1,0:T(4,128)(4,1)}, u32[]{:S(2)}) copy-start(pred[4,128]{1,0:T(4,128)(4,1)} %get-tuple-element.144) | copy-start | bytes 1540
  860.8 49.9 %all-to-all-start.13 = ((bf16[8,256,256]{2,1,0:T(8,128)(2,1)}), bf16[8,256,256]{2,1,0:T(8,128)(2,1)S(1)}, u32[]{:S(2)}, u32[]{:S(2)}) async-start(bf16[8,256,256]{2,1,0:T(8,128)(2,1)} %bitcast.277), calls=%async_computation.15 | async-start | bytes 2097152 | tf_op jit(solution)/shard_map/all_to_all | solution.py:172
  910.8 51.2 %all-to-all-start.7 = ((bf16[8,256,256]{1,2,0:T(8,128)(2,1)}), bf16[8,256,256]{1,2,0:T(8,128)(2,1)}, u32[]{:S(2)}, u32[]{:S(2)}) async-start(bf16[8,256,256]{1,2,0:T(8,128)(2,1)} %copy.109), calls=%async_computation.9 | async-start | bytes 2097152 | tf_op jit(solution)/shard_map/all_to_all | solution.py:172
  915.0 11.3 copy-start.8
  962.0 53.3 %all-to-all-start.9 = ((bf16[4,4096,128]{2,1,0:T(8,128)(2,1)}), bf16[4,4096,128]{2,1,0:T(8,128)(2,1)}, u32[]{:S(2)}, u32[]{:S(2)}) async-start(bf16[4,4096,128]{2,1,0:T(8,128)(2,1)} %bitcast_bitcast_fusion), calls=%async_computation.11 | async-start | bytes 8388608 | tf_op jit(solution)/shard_map/all_to_all | solution.py:172
  1015.3 26.8 %all-to-all-start.8 = ((bf16[4,64,2048]{2,1,0:T(8,128)(2,1)}), bf16[4,64,2048]{2,1,0:T(8,128)(2,1)}, u32[]{:S(2)}, u32[]{:S(2)}) async-start(bf16[4,64,2048]{2,1,0:T(8,128)(2,1)} %bitcast.278), calls=%async_computation.10 | async-start | bytes 2097152 | tf_op jit(solution)/shard_map/all_to_all | solution.py:172
  1042.1 59.4 %all-to-all-start.10 = ((bf16[32,128,128]{2,1,0:T(8,128)(2,1)}), bf16[32,128,128]{2,1,0:T(8,128)(2,1)S(1)}, u32[]{:S(2)}, u32[]{:S(2)}) async-start(bf16[32,128,128]{2,1,0:T(8,128)(2,1)} %bitcast.82), calls=%async_computation.12 | async-start | bytes 2097152 | tf_op jit(solution)/shard_map/all_to_all | solution.py:172
  1048.3 10.4 copy-start.12
  1056.8 8.1 collective-permute-start.1
  1102.9 107.1 %copy-start.4 = (f32[128,2048]{1,0:T(8,128)S(1)}, f32[128,2048]{1,0:T(8,128)}, u32[]{:S(2)}) copy-start(f32[128,2048]{1,0:T(8,128)} %get-tuple-element.119) | copy-start | bytes 3145732
  1113.1 99.5 %all-to-all-start.6 = ((bf16[4,64,2048]{2,1,0:T(8,128)(2,1)}), bf16[4,64,2048]{2,1,0:T(8,128)(2,1)}, u32[]{:S(2)}, u32[]{:S(2)}) async-start(bf16[4,64,2048]{2,1,0:T(8,128)(2,1)} %bitcast.274), calls=%async_computation.8 | async-start | bytes 2097152 | tf_op jit(solution)/shard_map/all_to_all | solution.py:172
  (4 other events, 4.5 us)
Sparse Core Ops, SparseCore 0:
  11.1 117.0 all-gather.7
  131.2 130.6 all-gather.9
  319.8 113.2 all-gather.11
  489.7 147.0 reduce-scatter.2
  663.0 112.5 all-gather.13
  778.5 134.8 all-gather.15
  917.1 189.3 reduce-scatter.4
